TPU v7x, 32 devices: a whole 2x2x4 slice. The times are simulated.
32 devices in a mesh: blk: 2 (over x), rows: 16 (over z, y, core).
Axes of the slice: x: 2, y: 2, z: 4, core: 2. Of those that a mesh axis runs over, the one named last changes fastest.
Arguments:
- features: bfloat16 [8192, 128], P(('blk', 'rows')), may hold values from -6 to 6
- labels: int32 [8192], P(('blk', 'rows')), may hold values from 0 to 6
- destination: int32 [8192, 1], P(('blk', 'rows')), may hold values from 0 to 15; in each aligned block of 256 rows (0 to 255, 256 to 511, ...) at most 32 rows name the same one
- centres: bfloat16 [8192, 128], P('blk'), may hold values from -6 to 6
- tri_inverse: float32 [8192, 8192], P('blk', 'rows'), may hold values from -1 to 2, as said below
- aux_inverse: float32 [8192, 8192], P('blk', 'rows'), may hold values from -1 to 2, as said below
Outputs:
- predictions: float32 [7, 16384], P(None, ('blk', 'rows'))
Inputs may be any that keep to these rules, and one draw needn't show every extreme that they name: `destination`: in each aligned block of 256 rows (the rows of one device) no value occurs more than 32 times, and some value occurs exactly 32 times. `tri_inverse`: zero below the diagonal, positive on it. `aux_inverse`: zero below the diagonal, positive on it.
All inputs are finite; a program needn't handle non-finite values.
Results may differ from a plain program's by a relative error of at most 0.0003.
Values may be sent and summed in bfloat16 or wider, within the bound.
A program may use at most 128 MiB of HBM per device.

v0:
```python
import math
import jax
import jax.numpy as jnp
from jax import lax
from jax.sharding import PartitionSpec as P

M = 8192
CLASSES = 7
ITERS = 2
ridge_weight = 0.1
highest = lax.Precision.HIGHEST


def vector_total(values):
    return lax.psum(values, ("blk", "rows"))


def square_norms(rows_x):
    return jnp.einsum("nd,nd->n", rows_x, rows_x, preferred_element_type=jnp.float32)


def kernel_tile(rows_x, rows_norm, centre_x, centre_norm, scale):
    inner = lax.dot_general(
        rows_x, centre_x, (((1,), (1,)), ((), ())), preferred_element_type=jnp.float32
    )
    return jnp.exp(-(rows_norm[:, None] + centre_norm[None, :] - 2.0 * inner) * scale).astype(
        jnp.bfloat16
    )


def against_rows(vector_low, tile):
    return lax.dot_general(
        vector_low, tile, (((1,), (1,)), ((), ())), preferred_element_type=jnp.float32
    )


def factor_forward(block, vector):
    block_rows, block_cols = block.shape
    ours = lax.dynamic_slice_in_dim(vector, lax.axis_index("rows") * block_cols, block_cols, 1)
    partial_rows = lax.dot_general(
        ours, block, (((1,), (1,)), ((), ())), precision=highest, preferred_element_type=jnp.float32
    )
    summed = lax.psum(partial_rows, "rows")
    return lax.all_gather(summed, "blk", axis=1, tiled=True)


def factor_backward(block, vector):
    block_rows, block_cols = block.shape
    ours = lax.dynamic_slice_in_dim(vector, lax.axis_index("blk") * block_rows, block_rows, 1)
    partial_cols = jnp.dot(ours, block, precision=highest, preferred_element_type=jnp.float32)
    summed = lax.psum(partial_cols, "blk")
    return lax.all_gather(summed, "rows", axis=1, tiled=True)


def class_targets(tags):
    class_ids = jnp.arange(CLASSES, dtype=jnp.float32)[:, None] + 1.0
    live = (tags > 0.5).astype(jnp.float32)
    return (live, live[None, :] * jnp.where(tags[None, :] == class_ids, 1.0, -1.0))


def on_device(features, labels, destination, centres, tri_inverse, aux_inverse):
    groups = lax.axis_size("rows")
    own_rows, width = features.shape
    capacity = max(2, 2 * own_rows // groups)
    scale = 2.0 / width
    count_all = float(own_rows * lax.axis_size("blk") * groups)
    target = destination[:, 0]
    picks = (target[:, None] == jnp.arange(groups, dtype=jnp.int32)[None, :]).astype(jnp.int32)
    before = jnp.sum((jnp.cumsum(picks, axis=0) - picks) * picks, axis=1)
    send_rows = jnp.zeros((groups, capacity, width), jnp.bfloat16).at[target, before].set(features)
    send_tags = (
        jnp.zeros((groups, capacity), jnp.bfloat16)
        .at[target, before]
        .set((labels + 1).astype(jnp.bfloat16))
    )
    got_rows, got_tags = (
        lax.all_to_all(send_rows, "rows", split_axis=0, concat_axis=0, tiled=True),
        lax.all_to_all(send_tags, "rows", split_axis=0, concat_axis=0, tiled=True),
    )
    slots = groups * capacity
    slot_rows = got_rows.reshape(slots, width)
    slot_tags = got_tags.reshape(slots)
    live, targets = class_targets(slot_tags.astype(jnp.float32))
    every_centre = lax.all_gather(centres, "blk", axis=0, tiled=True)
    centre_norm = square_norms(every_centre)
    block_rows = math.gcd(slots, 64)
    block_count = slots // block_rows
    stacked_rows = slot_rows.reshape(block_count, block_rows, width)
    stacked_live = live.reshape(block_count, block_rows)
    stacked_targets = (
        targets.astype(jnp.bfloat16).reshape(CLASSES, block_count, block_rows).transpose(1, 0, 2)
    )

    def tile_of(rows_x):
        return kernel_tile(rows_x, square_norms(rows_x), every_centre, centre_norm, scale)

    def gram_apply(vector):
        vector_low = vector.astype(jnp.bfloat16)

        def gram_visit(carry, pieces):
            rows_x, rows_live = pieces
            tile = tile_of(rows_x)
            image = (against_rows(vector_low, tile) * rows_live[None, :]).astype(jnp.bfloat16)
            return (carry + jnp.dot(image, tile, preferred_element_type=jnp.float32), None)

        partial_sum, _ = lax.scan(
            gram_visit, jnp.zeros((CLASSES, M), jnp.float32), (stacked_rows, stacked_live)
        )
        return vector_total(partial_sum) / count_all

    def kernel_visit(carry, pieces):
        rows_x, rows_targets = pieces
        return (
            carry + jnp.dot(rows_targets, tile_of(rows_x), preferred_element_type=jnp.float32),
            None,
        )

    partial_sum, _ = lax.scan(
        kernel_visit, jnp.zeros((CLASSES, M), jnp.float32), (stacked_rows, stacked_targets)
    )
    rhs = factor_backward(
        aux_inverse, factor_backward(tri_inverse, vector_total(partial_sum) / count_all)
    )
    solution = jnp.zeros((CLASSES, M), jnp.float32)
    residual = rhs
    direction = rhs
    norm_now = jnp.sum(residual * residual, axis=1, keepdims=True)
    for step in range(ITERS):
        first = factor_forward(aux_inverse, direction)
        second = factor_forward(tri_inverse, first)
        third = factor_backward(tri_inverse, gram_apply(second))
        image = factor_backward(aux_inverse, third + ridge_weight * first)
        step_size = norm_now / jnp.sum(direction * image, axis=1, keepdims=True)
        solution = solution + step_size * direction
        residual = residual - step_size * image
        norm_next = jnp.sum(residual * residual, axis=1, keepdims=True)
        direction = residual + norm_next / norm_now * direction
        norm_now = norm_next
    coefficients = factor_forward(tri_inverse, factor_forward(aux_inverse, solution))
    vector_low = coefficients.astype(jnp.bfloat16)
    scores = lax.map(lambda rows_x: against_rows(vector_low, tile_of(rows_x)), stacked_rows)
    return scores.transpose(1, 0, 2).reshape(CLASSES, slots) * live[None, :]


def solution(mesh):
    return jax.shard_map(
        on_device,
        mesh=mesh,
        in_specs=(
            P(("blk", "rows"), None),
            P(("blk", "rows")),
            P(("blk", "rows"), None),
            P("blk", None),
            P("blk", "rows"),
            P("blk", "rows"),
        ),
        out_specs=P(None, ("blk", "rows")),
        check_vma=False,
    )
```

profile of v0, /device:TPU:0, one launch (start us, length us, event | category | flops | bytes accessed | tf_op | source)
XLA Modules:
  0.0 1247.6 jit_solution(15171571763644554743)
XLA Ops:
  10.9 12.9 %scatter_fusion.1 = bf16[16,32]{1,0:T(8,128)(2,1)S(1)} fusion(bf16[16,32]{1,0:T(8,128)(2,1)S(1)} %broadcast_in_dim.21, s32[256]{0:T(256)S(1)} %bitcast.127, bf16[256]{0:T(256)(128)(2,1)S(1)} %add_convert_fusion), kind=kCustom, calls=%fused_computation.1 | custom fusion | bytes 3584 | tf_op jit(solution)/shard_map/scatter | solution.py:74
  32.5 27.0 %scatter_fusion = bf16[16,32,128]{2,1,0:T(8,128)(2,1)} fusion(bf16[16,32,128]{2,1,0:T(8,128)(2,1)} %broadcast_in_dim.20, s32[256]{0:T(256)S(1)} %bitcast.128, bf16[256,128]{1,0:T(8,128)(2,1)S(1)} %copy-done.5), kind=kCustom, calls=%fused_computation | custom fusion | bytes 198656 | tf_op jit(solution)/shard_map/scatter | solution.py:70
  83.3 122.6 %all-reduce.7.cloned.1.call-done = f32[7,8192]{1,0:T(8,128)} async-done(((f32[7,8192]{1,0:T(8,128)}), f32[7,8192]{1,0:T(8,128)}) %all-reduce.7.cloned.1.call-update) | async-done | bytes 229392 | tf_op jit(solution)/shard_map/psum | solution.py:15
  219.8 20.1 %all_gather.40 = f32[7,8192]{1,0:T(8,128)S(1)} all-gather(f32[7,512]{1,0:T(8,128)S(1)} %psum.106), channel_id=1, replica_groups=mesh['blk'=2,'rows'=16] {'rows'}, dimensions={1}, use_global_device_ids=true | all-gather | bytes 243712 | tf_op jit(solution)/shard_map/all_gather | solution.py:52
  253.6 17.8 %all_gather.41 = f32[7,8192]{1,0:T(8,128)S(1)} all-gather(f32[7,512]{1,0:T(8,128)S(1)} %psum.107), channel_id=1, replica_groups=mesh['blk'=2,'rows'=16] {'rows'}, dimensions={1}, use_global_device_ids=true | all-gather | bytes 243712 | tf_op jit(solution)/shard_map/all_gather | solution.py:52
  271.5 9.8 fusion.94
  281.4 85.0 %all-reduce.9.cloned.1.call-done = f32[7,4096]{1,0:T(8,128)} async-done(((f32[7,4096]{1,0:T(8,128)}), f32[7,4096]{1,0:T(8,128)}) %all-reduce.9.cloned.1.call-update) | async-done | bytes 114704 | tf_op jit(solution)/shard_map/psum | solution.py:43
  382.5 58.7 %psum.109 = bf16[7,4096]{1,0:T(8,128)(2,1)S(1)} all-reduce(f32[7,4096]{1,0:T(8,128)S(1)} %fusion.87), channel_id=1, replica_groups=mesh['blk'=2,'rows'=16] {'rows'}, use_global_device_ids=true, to_apply=%region_12.13 | all-reduce | flops 28672 | bytes 172032 | tf_op jit(solution)/shard_map/psum | solution.py:43
  446.1 28.1 %while.45 = (s32[]{:T(128)}, f32[7,8192]{1,0:T(8,128)S(1)}, bf16[8,64,128]{2,1,0:T(8,128)(2,1)S(1)}, f32[8192]{0:T(1024)S(1)}, bf16[8192,128]{1,0:T(8,128)(2,1)}...) while((s32[]{:T(128)}, f32[7,8192]{1,0:T(8,128)S(1)}, ...), condition=%wide.region_14.15_spmd.clone, body=%wide.region_13.14_spmd.clone.sunk | while | flops 152183616 | bytes 4834931 | solution.py:106
  475.0 122.3 %all-reduce.11.cloned.1.call-done = f32[7,8192]{1,0:T(8,128)} async-done(((f32[7,8192]{1,0:T(8,128)}), f32[7,8192]{1,0:T(8,128)}) %all-reduce.11.cloned.1.call-update) | async-done | bytes 229392 | tf_op jit(solution)/shard_map/psum | solution.py:15
  611.1 20.1 %all_gather.44 = f32[7,8192]{1,0:T(8,128)S(1)} all-gather(f32[7,512]{1,0:T(8,128)S(1)} %psum.111), channel_id=1, replica_groups=mesh['blk'=2,'rows'=16] {'rows'}, dimensions={1}, use_global_device_ids=true | all-gather | bytes 243712 | tf_op jit(solution)/shard_map/all_gather | solution.py:52
  645.0 17.8 %all_gather.45 = f32[7,8192]{1,0:T(8,128)S(1)} all-gather(f32[7,512]{1,0:T(8,128)S(1)} %psum.112), channel_id=1, replica_groups=mesh['blk'=2,'rows'=16] {'rows'}, dimensions={1}, use_global_device_ids=true | all-gather | bytes 243712 | tf_op jit(solution)/shard_map/all_gather | solution.py:52
  663.4 9.8 fusion.91
  673.3 85.0 %all-reduce.13.cloned.1.call-done = f32[7,4096]{1,0:T(8,128)} async-done(((f32[7,4096]{1,0:T(8,128)}), f32[7,4096]{1,0:T(8,128)}) %all-reduce.13.cloned.1.call-update) | async-done | bytes 114704 | tf_op jit(solution)/shard_map/psum | solution.py:43
  774.2 58.7 %psum.114 = bf16[7,4096]{1,0:T(8,128)(2,1)S(1)} all-reduce(f32[7,4096]{1,0:T(8,128)S(1)} %fusion.84), channel_id=1, replica_groups=mesh['blk'=2,'rows'=16] {'rows'}, use_global_device_ids=true, to_apply=%region_21.22 | all-reduce | flops 28672 | bytes 172032 | tf_op jit(solution)/shard_map/psum | solution.py:43
  837.8 28.1 %while.46 = (s32[]{:T(128)}, f32[7,8192]{1,0:T(8,128)S(1)}, bf16[8,64,128]{2,1,0:T(8,128)(2,1)S(1)}, f32[8192]{0:T(1024)S(1)}, bf16[8192,128]{1,0:T(8,128)(2,1)}...) while((s32[]{:T(128)}, f32[7,8192]{1,0:T(8,128)S(1)}, ...), condition=%wide.region_23.24_spmd.clone, body=%wide.region_22.23_spmd.clone.sunk | while | flops 152183616 | bytes 4834931 | solution.py:106
  866.6 122.3 %all-reduce.15.cloned.1.call-done = f32[7,8192]{1,0:T(8,128)} async-done(((f32[7,8192]{1,0:T(8,128)}), f32[7,8192]{1,0:T(8,128)}) %all-reduce.15.cloned.1.call-update) | async-done | bytes 229392 | tf_op jit(solution)/shard_map/psum | solution.py:15
  1002.7 20.1 %all_gather.48 = f32[7,8192]{1,0:T(8,128)S(1)} all-gather(f32[7,512]{1,0:T(8,128)S(1)} %psum.116), channel_id=1, replica_groups=mesh['blk'=2,'rows'=16] {'rows'}, dimensions={1}, use_global_device_ids=true | all-gather | bytes 243712 | tf_op jit(solution)/shard_map/all_gather | solution.py:52
  1036.6 17.8 %all_gather.49 = f32[7,8192]{1,0:T(8,128)S(1)} all-gather(f32[7,512]{1,0:T(8,128)S(1)} %psum.117), channel_id=1, replica_groups=mesh['blk'=2,'rows'=16] {'rows'}, dimensions={1}, use_global_device_ids=true | all-gather | bytes 243712 | tf_op jit(solution)/shard_map/all_gather | solution.py:52
  1054.6 9.8 fusion.81
  1064.5 84.9 %all-reduce.17.cloned.1.call-done = f32[7,4096]{1,0:T(8,128)} async-done(((f32[7,4096]{1,0:T(8,128)}), f32[7,4096]{1,0:T(8,128)}) %all-reduce.17.cloned.1.call-update) | async-done | bytes 114704 | tf_op jit(solution)/shard_map/psum | solution.py:43
  1156.3 9.3 fusion.79
  1165.6 58.7 %psum.119 = bf16[7,4096]{1,0:T(8,128)(2,1)S(1)} all-reduce(f32[7,4096]{1,0:T(8,128)S(1)} %fusion.79), channel_id=1, replica_groups=mesh['blk'=2,'rows'=16] {'rows'}, use_global_device_ids=true, to_apply=%region_29.30 | all-reduce | flops 28672 | bytes 172032 | tf_op jit(solution)/shard_map/psum | solution.py:43
  1229.2 10.7 while.43
  (180 shorter events, 251.5 us)
Async XLA Ops:
  6.5 26.0 %copy-start.5 = (bf16[256,128]{1,0:T(8,128)(2,1)S(1)}, bf16[256,128]{1,0:T(8,128)(2,1)}, u32[]{:S(2)}) copy-start(bf16[256,128]{1,0:T(8,128)(2,1)} %param.14) | copy-start | bytes 196612
  6.5 59.1 %all-gather.2.cloned.1.call-start = ((), (), s32[]{:S(2)}) async-start(), calls=%async_computation.2 | async-start | bytes 3145728 | tf_op jit(solution)/shard_map/all_gather | solution.py:84
  24.5 35.1 %all-to-all-start.1 = ((bf16[16,1,32]{2,1,0:T(2,128)(2,1)}), bf16[16,1,32]{2,1,0:T(2,128)(2,1)S(1)}, u32[]{:S(2)}, u32[]{:S(2)}) async-start(bf16[16,1,32]{2,1,0:T(2,128)(2,1)} %copy.11), calls=%async_computation.1 | async-start | bytes 16384 | tf_op jit(solution)/shard_map/all_to_all | solution.py:78
  59.5 13.8 %all-to-all-start = ((bf16[16,32,128]{2,1,0:T(8,128)(2,1)}), bf16[16,32,128]{2,1,0:T(8,128)(2,1)S(1)}, u32[]{:S(2)}, u32[]{:S(2)}) async-start(bf16[16,32,128]{2,1,0:T(8,128)(2,1)} %scatter_fusion), calls=%async_computation | async-start | bytes 262144 | tf_op jit(solution)/shard_map/all_to_all | solution.py:77
  65.4 140.6 %all-reduce.7.cloned.1.call-start = ((), (), s32[]{:S(2)}) async-start(), calls=%async_computation.3 | async-start | bytes 524288 | tf_op jit(solution)/shard_map/psum | solution.py:15
  65.6 7.7 copy-start.2
  82.5 0.7 copy-start.4
  83.2 283.1 %all-reduce.9.cloned.1.call-start = ((), (), s32[]{:S(2)}) async-start(), calls=%async_computation.4 | async-start | bytes 262144 | tf_op jit(solution)/shard_map/psum | solution.py:43
  281.3 316.0 %all-reduce.11.cloned.1.call-start = ((), (), s32[]{:S(2)}) async-start(), calls=%async_computation.5 | async-start | bytes 524288 | tf_op jit(solution)/shard_map/psum | solution.py:15
  474.2 0.7 copy-start
  474.9 283.3 %all-reduce.13.cloned.1.call-start = ((), (), s32[]{:S(2)}) async-start(), calls=%async_computation.6 | async-start | bytes 262144 | tf_op jit(solution)/shard_map/psum | solution.py:43
  673.3 315.7 %all-reduce.15.cloned.1.call-start = ((), (), s32[]{:S(2)}) async-start(), calls=%async_computation.7 | async-start | bytes 524288 | tf_op jit(solution)/shard_map/psum | solution.py:15
  865.9 0.7 copy-start.1
  866.6 282.9 %all-reduce.17.cloned.1.call-start = ((), (), s32[]{:S(2)}) async-start(), calls=%async_computation.8 | async-start | bytes 262144 | tf_op jit(solution)/shard_map/psum | solution.py:43
  1156.3 72.9 %copy-start.3 = (bf16[8192,128]{1,0:T(8,128)(2,1)S(1)}, bf16[8192,128]{1,0:T(8,128)(2,1)}, u32[]{:S(2)}) copy-start(bf16[8192,128]{1,0:T(8,128)(2,1)} %get-tuple-element.545) | copy-start | bytes 6291460
Sparse Core Ops, SparseCore 0:
  8.9 35.8 all-gather.1
  83.4 122.5 all-reduce.6
  281.4 84.8 all-reduce.8
  475.1 122.1 all-reduce.10
  673.4 84.8 all-reduce.12
  866.7 122.1 all-reduce.14
  1064.6 84.8 all-reduce.16
where the time goes:
time: 1260 us; the launch traced here: 1250 us
  waiting for transfers between devices  628 us (50%)
  blocking collectives  374 us (30%)
  matrix products  163 us (13%)
  local copies, waits for them, and re-layouts  43.9 us (3%)
  between operations  13.9 us (1%)
  starting transfers between devices  13.5 us (1%)
    psum x3, waiting for transfers between devices, vector_total(): return lax.psum(values, ('blk', 'rows'))  367 us
    psum x3, waiting for transfers between devices, factor_forward(): summed = lax.psum(partial_rows, 'rows')  255 us
    psum x3, blocking collectives, factor_forward(): summed = lax.psum(partial_rows, 'rows')  176 us
    all_gather x6, blocking collectives, factor_backward(): return lax.all_gather(summed, 'rows', axis=1, tiled=True)  114 us
    dot_general x6, matrix products, factor_forward(): lax.dot_general(ours, block, (((1,), (1,)), ((), ())), precision=highest,...  57 us
    psum x6, blocking collectives, factor_backward(): summed = lax.psum(partial_cols, 'blk')  48.5 us
    dot_general x16, matrix products, kernel_tile(): lax.dot_general(rows_x, centre_x, (((1,), (1,)), ((), ())), preferred_ele...  39.3 us
    all_gather x6, blocking collectives, factor_forward(): return lax.all_gather(summed, 'blk', axis=1, tiled=True)  35.4 us
  transfers between devices with their start and end apart: 9, of which 7 were waited for; matrix products, arithmetic and copies ran while one was open for 4% of the time, Pallas kernels for 0%

commit v1 on v0

--- a/solution.py
+++ b/solution.py
@@ -3,6 +3,7 @@
 import jax.numpy as jnp
 from jax import lax
 from jax.sharding import PartitionSpec as P
+from jax.lax import all_gather
 
 M = 8192
 CLASSES = 7
@@ -11,8 +12,12 @@
 highest = lax.Precision.HIGHEST
 
 
+def domain_clear(xin, across):
+    return all_gather(xin, axis_name=across).sum(axis=0)
+
+
 def vector_total(values):
-    return lax.psum(values, ("blk", "rows"))
+    return domain_clear(values, ("blk", "rows"))
 
 
 def square_norms(rows_x):

time: 1260 us -> 1120 us (0.89)
  waiting for transfers between devices: 628 us -> 486 us
    psum x3 -> x0, waiting for transfers between devices: 367 us -> none  [vector_total(): return lax.psum(values, ('blk', 'rows'))]
    all_gather x0 -> x3, waiting for transfers between devices: none -> 225 us  [domain_clear(): return all_gather(xin, axis_name=across).sum(axis=0)]
where the time goes in v1:
time: 1120 us
  waiting for transfers between devices  486 us (43%)
  blocking collectives  373 us (33%)
  matrix products  163 us (15%)
  local copies, waits for them, and re-layouts  43.8 us (4%)
  other arithmetic  23.5 us (2%)
  between operations  13.9 us (1%)
  starting transfers between devices  13.8 us (1%)
    psum x3, waiting for transfers between devices, factor_forward(): summed = lax.psum(partial_rows, 'rows')  255 us
    all_gather x3, waiting for transfers between devices, domain_clear(): return all_gather(xin, axis_name=across).sum(axis=0)  225 us
    psum x3, blocking collectives, factor_forward(): summed = lax.psum(partial_rows, 'rows')  176 us
    all_gather x6, blocking collectives, factor_backward(): return lax.all_gather(summed, 'rows', axis=1, tiled=True)  113 us
    dot_general x6, matrix products, factor_forward(): lax.dot_general(ours, block, (((1,), (1,)), ((), ())), precision=highest,...  57 us
    psum x6, blocking collectives, factor_backward(): summed = lax.psum(partial_cols, 'blk')  48.7 us
    dot_general x16, matrix products, kernel_tile(): lax.dot_general(rows_x, centre_x, (((1,), (1,)), ((), ())), preferred_ele...  39.3 us
    all_gather x6, blocking collectives, factor_forward(): return lax.all_gather(summed, 'blk', axis=1, tiled=True)  34.6 us
  transfers between devices with their start and end apart: 9, of which 7 were waited for; matrix products, arithmetic and copies ran while one was open for 4% of the time, Pallas kernels for 0%

profile of v1, /device:TPU:0, one launch (start us, length us, event | category | flops | bytes accessed | tf_op | source)
XLA Modules:
  0.0 1116.6 jit_solution(15179929521406327332)
XLA Ops:
  10.9 12.9 %scatter_fusion.1 = bf16[16,32]{1,0:T(8,128)(2,1)S(1)} fusion(bf16[16,32]{1,0:T(8,128)(2,1)S(1)} %broadcast_in_dim.21, s32[256]{0:T(256)S(1)} %bitcast.130, bf16[256]{0:T(256)(128)(2,1)S(1)} %add_convert_fusion), kind=kCustom, calls=%fused_computation.1 | custom fusion | bytes 3584 | tf_op jit(solution)/shard_map/scatter | solution.py:79
  32.5 26.9 %scatter_fusion = bf16[16,32,128]{2,1,0:T(8,128)(2,1)} fusion(bf16[16,32,128]{2,1,0:T(8,128)(2,1)} %broadcast_in_dim.20, s32[256]{0:T(256)S(1)} %bitcast.131, bf16[256,128]{1,0:T(8,128)(2,1)S(1)} %copy-done.5), kind=kCustom, calls=%fused_computation | custom fusion | bytes 198656 | tf_op jit(solution)/shard_map/scatter | solution.py:75
  83.3 75.2 %all-gather.13.cloned.1.call-done = f32[32,7,8192]{2,1,0:T(8,128)} async-done(((f32[1,7,8192]{2,1,0:T(8,128)}), f32[32,7,8192]{2,1,0:T(8,128)}) %all-gather.13.cloned.1.call-update) | async-done | bytes 7340048 | tf_op jit(solution)/shard_map/all_gather | solution.py:16
  176.3 19.7 %all_gather.60 = f32[7,8192]{1,0:T(8,128)S(1)} all-gather(f32[7,512]{1,0:T(8,128)S(1)} %psum.84), channel_id=1, replica_groups=mesh['blk'=2,'rows'=16] {'rows'}, dimensions={1}, use_global_device_ids=true | all-gather | bytes 243712 | tf_op jit(solution)/shard_map/all_gather | solution.py:57
  209.8 18.3 %all_gather.61 = f32[7,8192]{1,0:T(8,128)S(1)} all-gather(f32[7,512]{1,0:T(8,128)S(1)} %psum.85), channel_id=1, replica_groups=mesh['blk'=2,'rows'=16] {'rows'}, dimensions={1}, use_global_device_ids=true | all-gather | bytes 243712 | tf_op jit(solution)/shard_map/all_gather | solution.py:57
  228.1 9.8 fusion.94
  238.0 85.1 %all-reduce.4.cloned.1.call-done = f32[7,4096]{1,0:T(8,128)} async-done(((f32[7,4096]{1,0:T(8,128)}), f32[7,4096]{1,0:T(8,128)}) %all-reduce.4.cloned.1.call-update) | async-done | bytes 114704 | tf_op jit(solution)/shard_map/psum | solution.py:48
  338.8 58.7 %psum.87 = bf16[7,4096]{1,0:T(8,128)(2,1)S(1)} all-reduce(f32[7,4096]{1,0:T(8,128)S(1)} %fusion.87), channel_id=1, replica_groups=mesh['blk'=2,'rows'=16] {'rows'}, use_global_device_ids=true, to_apply=%region_12.13 | all-reduce | flops 28672 | bytes 172032 | tf_op jit(solution)/shard_map/psum | solution.py:48
  402.4 28.1 %while.45 = (s32[]{:T(128)}, f32[7,8192]{1,0:T(8,128)S(1)}, bf16[8,64,128]{2,1,0:T(8,128)(2,1)S(1)}, f32[8192]{0:T(1024)S(1)}, bf16[8192,128]{1,0:T(8,128)(2,1)}...) while((s32[]{:T(128)}, f32[7,8192]{1,0:T(8,128)S(1)}, ...), condition=%wide.region_14.15_spmd.clone, body=%wide.region_13.14_spmd.clone.sunk | while | flops 152183616 | bytes 4834931 | solution.py:111
  431.3 74.9 %all-gather.15.cloned.1.call-done = f32[32,7,8192]{2,1,0:T(8,128)} async-done(((f32[1,7,8192]{2,1,0:T(8,128)}), f32[32,7,8192]{2,1,0:T(8,128)}) %all-gather.15.cloned.1.call-update) | async-done | bytes 7340048 | tf_op jit(solution)/shard_map/all_gather | solution.py:16
  524.0 19.9 %all_gather.66 = f32[7,8192]{1,0:T(8,128)S(1)} all-gather(f32[7,512]{1,0:T(8,128)S(1)} %psum.88), channel_id=1, replica_groups=mesh['blk'=2,'rows'=16] {'rows'}, dimensions={1}, use_global_device_ids=true | all-gather | bytes 243712 | tf_op jit(solution)/shard_map/all_gather | solution.py:57
  557.8 17.8 %all_gather.67 = f32[7,8192]{1,0:T(8,128)S(1)} all-gather(f32[7,512]{1,0:T(8,128)S(1)} %psum.89), channel_id=1, replica_groups=mesh['blk'=2,'rows'=16] {'rows'}, dimensions={1}, use_global_device_ids=true | all-gather | bytes 243712 | tf_op jit(solution)/shard_map/all_gather | solution.py:57
  576.2 9.8 fusion.91
  586.1 85.1 %all-reduce.6.cloned.1.call-done = f32[7,4096]{1,0:T(8,128)} async-done(((f32[7,4096]{1,0:T(8,128)}), f32[7,4096]{1,0:T(8,128)}) %all-reduce.6.cloned.1.call-update) | async-done | bytes 114704 | tf_op jit(solution)/shard_map/psum | solution.py:48
  686.9 58.7 %psum.91 = bf16[7,4096]{1,0:T(8,128)(2,1)S(1)} all-reduce(f32[7,4096]{1,0:T(8,128)S(1)} %fusion.84), channel_id=1, replica_groups=mesh['blk'=2,'rows'=16] {'rows'}, use_global_device_ids=true, to_apply=%region_21.22 | all-reduce | flops 28672 | bytes 172032 | tf_op jit(solution)/shard_map/psum | solution.py:48
  750.5 28.1 %while.46 = (s32[]{:T(128)}, f32[7,8192]{1,0:T(8,128)S(1)}, bf16[8,64,128]{2,1,0:T(8,128)(2,1)S(1)}, f32[8192]{0:T(1024)S(1)}, bf16[8192,128]{1,0:T(8,128)(2,1)}...) while((s32[]{:T(128)}, f32[7,8192]{1,0:T(8,128)S(1)}, ...), condition=%wide.region_23.24_spmd.clone, body=%wide.region_22.23_spmd.clone.sunk | while | flops 152183616 | bytes 4834931 | solution.py:111
  779.6 74.7 %all-gather.17.cloned.1.call-done = f32[32,7,8192]{2,1,0:T(8,128)} async-done(((f32[1,7,8192]{2,1,0:T(8,128)}), f32[32,7,8192]{2,1,0:T(8,128)}) %all-gather.17.cloned.1.call-update) | async-done | bytes 7340048 | tf_op jit(solution)/shard_map/all_gather | solution.py:16
  872.1 19.7 %all_gather.72 = f32[7,8192]{1,0:T(8,128)S(1)} all-gather(f32[7,512]{1,0:T(8,128)S(1)} %psum.92), channel_id=1, replica_groups=mesh['blk'=2,'rows'=16] {'rows'}, dimensions={1}, use_global_device_ids=true | all-gather | bytes 243712 | tf_op jit(solution)/shard_map/all_gather | solution.py:57
  905.7 17.8 %all_gather.73 = f32[7,8192]{1,0:T(8,128)S(1)} all-gather(f32[7,512]{1,0:T(8,128)S(1)} %psum.93), channel_id=1, replica_groups=mesh['blk'=2,'rows'=16] {'rows'}, dimensions={1}, use_global_device_ids=true | all-gather | bytes 243712 | tf_op jit(solution)/shard_map/all_gather | solution.py:57
  923.7 9.8 fusion.81
  933.6 85.1 %all-reduce.8.cloned.1.call-done = f32[7,4096]{1,0:T(8,128)} async-done(((f32[7,4096]{1,0:T(8,128)}), f32[7,4096]{1,0:T(8,128)}) %all-reduce.8.cloned.1.call-update) | async-done | bytes 114704 | tf_op jit(solution)/shard_map/psum | solution.py:48
  1025.3 9.3 fusion.79
  1034.6 58.7 %psum.95 = bf16[7,4096]{1,0:T(8,128)(2,1)S(1)} all-reduce(f32[7,4096]{1,0:T(8,128)S(1)} %fusion.79), channel_id=1, replica_groups=mesh['blk'=2,'rows'=16] {'rows'}, use_global_device_ids=true, to_apply=%region_29.30 | all-reduce | flops 28672 | bytes 172032 | tf_op jit(solution)/shard_map/psum | solution.py:48
  1098.2 10.7 while.43
  (183 shorter events, 263.4 us)
Async XLA Ops:
  6.5 26.0 %copy-start.5 = (bf16[256,128]{1,0:T(8,128)(2,1)S(1)}, bf16[256,128]{1,0:T(8,128)(2,1)}, u32[]{:S(2)}) copy-start(bf16[256,128]{1,0:T(8,128)(2,1)} %param.14) | copy-start | bytes 196612
  6.5 59.1 %all-gather.11.cloned.1.call-start = ((), (), s32[]{:S(2)}) async-start(), calls=%async_computation.2 | async-start | bytes 3145728 | tf_op jit(solution)/shard_map/all_gather | solution.py:89
  24.5 34.9 %all-to-all-start.1 = ((bf16[16,1,32]{2,1,0:T(2,128)(2,1)}), bf16[16,1,32]{2,1,0:T(2,128)(2,1)S(1)}, u32[]{:S(2)}, u32[]{:S(2)}) async-start(bf16[16,1,32]{2,1,0:T(2,128)(2,1)} %copy.11), calls=%async_computation.1 | async-start | bytes 16384 | tf_op jit(solution)/shard_map/all_to_all | solution.py:83
  59.4 13.9 %all-to-all-start = ((bf16[16,32,128]{2,1,0:T(8,128)(2,1)}), bf16[16,32,128]{2,1,0:T(8,128)(2,1)S(1)}, u32[]{:S(2)}, u32[]{:S(2)}) async-start(bf16[16,32,128]{2,1,0:T(8,128)(2,1)} %scatter_fusion), calls=%async_computation | async-start | bytes 262144 | tf_op jit(solution)/shard_map/all_to_all | solution.py:82
  65.3 93.1 %all-gather.13.cloned.1.call-start = ((), (), s32[]{:S(2)}) async-start(), calls=%async_computation.6 | async-start | bytes 8650752 | tf_op jit(solution)/shard_map/all_gather | solution.py:16
  65.6 7.7 copy-start.2
  82.5 0.7 copy-start.4
  83.2 239.9 %all-reduce.4.cloned.1.call-start = ((), (), s32[]{:S(2)}) async-start(), calls=%async_computation.3 | async-start | bytes 262144 | tf_op jit(solution)/shard_map/psum | solution.py:48
  237.9 268.3 %all-gather.15.cloned.1.call-start = ((), (), s32[]{:S(2)}) async-start(), calls=%async_computation.7 | async-start | bytes 8650752 | tf_op jit(solution)/shard_map/all_gather | solution.py:16
  430.5 0.7 copy-start
  431.3 239.9 %all-reduce.6.cloned.1.call-start = ((), (), s32[]{:S(2)}) async-start(), calls=%async_computation.4 | async-start | bytes 262144 | tf_op jit(solution)/shard_map/psum | solution.py:48
  586.0 268.3 %all-gather.17.cloned.1.call-start = ((), (), s32[]{:S(2)}) async-start(), calls=%async_computation.8 | async-start | bytes 8650752 | tf_op jit(solution)/shard_map/all_gather | solution.py:16
  778.6 0.7 copy-start.1
  779.4 239.3 %all-reduce.8.cloned.1.call-start = ((), (), s32[]{:S(2)}) async-start(), calls=%async_computation.5 | async-start | bytes 262144 | tf_op jit(solution)/shard_map/psum | solution.py:48
  1025.3 72.9 %copy-start.3 = (bf16[8192,128]{1,0:T(8,128)(2,1)S(1)}, bf16[8192,128]{1,0:T(8,128)(2,1)}, u32[]{:S(2)}) copy-start(bf16[8192,128]{1,0:T(8,128)(2,1)} %get-tuple-element.548) | copy-start | bytes 6291460
Sparse Core Ops, SparseCore 0:
  8.9 35.8 all-gather.10
  83.4 75.0 all-gather.12
  238.1 84.9 all-reduce.3
  431.4 74.7 all-gather.14
  586.2 84.9 all-reduce.5
  779.5 74.7 all-gather.16
  933.6 84.9 all-reduce.7
